TPU v7x, 256 devices: a whole 4x4x8 slice. The times are simulated.
256 devices in a mesh: row: 8 (over x, core), col: 32 (over y, z).
Axes of the slice: x: 4, y: 4, z: 8, core: 2. Of those that a mesh axis runs over, the one named last changes fastest.
Arguments:
- deflation: bfloat16 [16, 256, 16, 3072], P('row', 'col'), may hold values from 0 to 0.019897461
- coefficient: float32 [16, 256, 16], P('row', 'col'), may hold values from 1 to 10
- gradients: bfloat16 [3, 64, 64], replicated, may hold values from -0.75 to 0.75
- x_penalty: float32 [24, 256, 16], P('row', 'col'), may hold values from 1 to 10, as said below
- y_penalty: float32 [16, 288, 16], P('row', 'col'), may hold values from 1 to 10, as said below
- z_penalty: float32 [16, 256, 17], P('row', 'col'), may hold values from 1 to 10
- coarse_order: int32 [1024], replicated, may hold values from 0 to 1023, as said below
Outputs:
- coarse_blocks: float32 [1024, 7, 2304], P(('row', 'col'))
- panel: float32 [1024, 48, 528], P(('row', 'col'))
Inputs may be any that keep to these rules, and one draw needn't show every extreme that they name: `coarse_order`: each subdomain number appears once; subdomains with consecutive coarse numbers are mostly neighbours along the third or second dimension. `x_penalty`: row i * 3 + 2 equals row (i + 1) * 3: a face between two devices' blocks is held by both. `y_penalty`: column j * 9 + 8 equals column (j + 1) * 9: a face between two devices' blocks is held by both.
All inputs are finite; a program needn't handle non-finite values.
Results may differ from a plain program's by a relative error of at most 0.00044.
Values may be sent and summed in bfloat16 or wider, within the bound.
No kernel may reach another device: no remote copies, remote signals or barrier semaphores. Data moves between devices by JAX's collectives and lax.ppermute only.
A program may use at most 128 MiB of HBM per device.

v0:
```python
import jax
import jax.numpy as jnp
from jax import lax
from jax.sharding import PartitionSpec as P

NV = 48
SUB_DEV = 4
PB = 11
LINE_WEIGHTS = (1.0 / 6.0, 5.0 / 6.0, 5.0 / 6.0, 1.0 / 6.0)


def with_halo(shard, sides, width):
    for axis, dim in sides:
        size, length = (lax.axis_size(axis), shard.shape[dim])
        up = [(i, (i + 1) % size) for i in range(size - 1)]
        down = [(j, i) for i, j in up]
        last = lax.slice_in_dim(shard, length - width, length, axis=dim)
        initial = lax.slice_in_dim(shard, 0, width, axis=dim)
        before = lax.ppermute(last, axis, up)
        after = lax.ppermute(initial, axis, down)
        shard = jnp.concatenate([before, shard, after], axis=dim)
    return shard


def node_weights():
    line = jnp.array(LINE_WEIGHTS, jnp.float32)
    return (line[:, None, None] * line[None, :, None] * line[None, None, :]).reshape(64)


def contract(form, left, right):
    return jnp.einsum(form, left, right, preferred_element_type=jnp.float32)


def traces(values, axis, side):
    lead = values.ndim - 1
    nodes = values.reshape(values.shape[:lead] + (4, 4, 4, NV))
    picked = lax.index_in_dim(nodes, side, lead + axis, keepdims=False)
    return picked.reshape(values.shape[:lead] + (16, NV))


def scaled(trace, root):
    return (root[..., None, None] * trace.astype(jnp.float32)).astype(jnp.bfloat16)


def grouped(left, right, groups):
    shape = left.shape
    split = shape[:2] + (groups, shape[2] // groups) + shape[3:]
    return contract("xyskav,xyskaw->svw", left.reshape(split), right.reshape(split))


def lateral(plus, minus, root, below, above, groups):
    jump = (
        root[1:-1, :, :, None, None]
        * (plus[:-1].astype(jnp.float32) - minus[1:].astype(jnp.float32))
    ).astype(jnp.bfloat16)
    low_own = scaled(minus[0], root[0])
    low_other = scaled(below, root[0])
    high_own = scaled(plus[-1], root[-1])
    high_other = scaled(above, root[-1])
    self_part = (
        grouped(jump, jump, groups)
        + grouped(low_own[None], low_own[None], groups)
        + grouped(high_own[None], high_own[None], groups)
    )
    return (
        self_part,
        -grouped(low_own[None], low_other[None], groups),
        -grouped(high_own[None], high_other[None], groups),
    )


def vertical(plus, minus, root, groups):
    width, length, depth = plus.shape[:3]
    height = depth // groups
    plus = plus.reshape(width, length, groups, height, 16, NV)
    minus = minus.reshape(width, length, groups, height, 16, NV)
    inner_root = root[:, :, :depth].reshape(width, length, groups, height)[:, :, :, 1:]
    jump = (
        inner_root[..., None, None]
        * (plus[:, :, :, :-1].astype(jnp.float32) - minus[:, :, :, 1:].astype(jnp.float32))
    ).astype(jnp.bfloat16)
    edge_root = root[:, :, ::height]
    first = minus[:, :, :, 0]
    last = plus[:, :, :, -1]
    blank = jnp.zeros_like(last[:, :, :1])
    low_own = scaled(first, edge_root[:, :, :groups])
    low_other = scaled(jnp.concatenate([blank, last[:, :, :-1]], axis=2), edge_root[:, :, :groups])
    high_own = scaled(last, edge_root[:, :, 1:])
    high_other = scaled(jnp.concatenate([first[:, :, 1:], blank], axis=2), edge_root[:, :, 1:])
    pairing = "xysav,xysaw->svw"
    self_part = (
        contract("xyskav,xyskaw->svw", jump, jump)
        + contract(pairing, low_own, low_own)
        + contract(pairing, high_own, high_own)
    )
    return (
        self_part,
        -contract(pairing, low_own, low_other),
        -contract(pairing, high_own, high_other),
    )


def volume(values, coefficient, gradients, groups):
    width, length, depth = values.shape[:3]
    nodes = values.reshape(width, length, depth, 64, NV)
    factor = jnp.sqrt(coefficient[..., None] * node_weights())
    total = jnp.zeros((groups, NV, NV), jnp.float32)
    for axis in range(3):
        product = contract("ab,xyzbv->xyzav", gradients[axis], nodes)
        rounded = (product * factor[..., None]).astype(jnp.bfloat16)
        rounded = rounded.reshape(width, length, groups, depth // groups, 64, NV)
        total = total + contract("xyskav,xyskaw->svw", rounded, rounded)
    return total


def panel_rows(blocks, column_block, present):
    picks = (
        present[:, :, None]
        & (column_block[:, :, None] == jnp.arange(PB, dtype=jnp.int32)[None, None, :])
    ).astype(jnp.float32)
    rows = jnp.einsum("stp,stvw->svpw", picks, blocks, precision=lax.Precision.HIGHEST).reshape(
        blocks.shape[0], NV, PB * NV
    )
    select = (column_block[:, :1] == jnp.arange(PB, dtype=jnp.int32)[None, :]).astype(jnp.float32)
    share = jnp.einsum("sp,svq->pvq", select, rows, precision=lax.Precision.HIGHEST)
    return (rows, select, share)


def finish(rows, select, assembled):
    whole = assembled.reshape(PB * NV, PB * NV)
    factor = jnp.linalg.cholesky(0.5 * (whole + whole.T))
    count = rows.shape[0]
    solved = jax.scipy.linalg.solve_triangular(
        factor, rows.reshape(count * NV, PB * NV).T, lower=True
    ).T.reshape(count, NV, PB * NV)
    inside = jnp.einsum(
        "sp,pvq->svq", select, factor.reshape(PB, NV, PB * NV), precision=lax.Precision.HIGHEST
    )
    return jnp.where(jnp.sum(select, axis=1)[:, None, None] > 0, inside, solved)


def shards(deflation, coefficient, gradients, x_penalty, y_penalty, z_penalty, coarse_order):
    plus_x = traces(deflation, 0, 3)
    minus_x = traces(deflation, 0, 0)
    plus_y = traces(deflation, 1, 3)
    minus_y = traces(deflation, 1, 0)
    padded = with_halo(deflation, (("row", 0), ("col", 1)), 1)
    below_x = traces(padded[0, 1:-1], 0, 3)
    above_x = traces(padded[-1, 1:-1], 0, 0)
    below_y = traces(padded[1:-1, 0], 1, 3)
    above_y = traces(padded[1:-1, -1], 1, 0)
    x_root = jnp.sqrt(x_penalty)
    y_root = jnp.sqrt(y_penalty)
    z_root = jnp.sqrt(z_penalty)
    self_x, low_x, high_x = lateral(plus_x, minus_x, x_root, below_x, above_x, SUB_DEV)
    self_y, low_y, high_y = lateral(
        jnp.swapaxes(plus_y, 0, 1),
        jnp.swapaxes(minus_y, 0, 1),
        jnp.swapaxes(y_root, 0, 1),
        below_y,
        above_y,
        SUB_DEV,
    )
    self_z, low_z, high_z = vertical(
        traces(deflation, 2, 3), traces(deflation, 2, 0), z_root, SUB_DEV
    )
    diagonal = volume(deflation, coefficient, gradients, SUB_DEV) + self_x + self_y + self_z
    blocks = jnp.stack([diagonal, low_x, high_x, low_y, high_y, low_z, high_z], axis=1)
    row_pos = lax.axis_index("row")
    col_pos = lax.axis_index("col")
    row_count = lax.axis_size("row")
    col_count = lax.axis_size("col")
    device = row_pos * col_count + col_pos
    local = jnp.arange(SUB_DEV, dtype=jnp.int32)
    owner = device * SUB_DEV + local
    stride = col_count * SUB_DEV
    neighbours = jnp.stack(
        [
            owner,
            owner - stride,
            owner + stride,
            owner - SUB_DEV,
            owner + SUB_DEV,
            owner - 1,
            owner + 1,
        ],
        axis=1,
    )
    always = jnp.ones((SUB_DEV,), bool)
    present = jnp.stack(
        [
            always,
            always & (row_pos > 0),
            always & (row_pos < row_count - 1),
            always & (col_pos > 0),
            always & (col_pos < col_count - 1),
            local > 0,
            local < SUB_DEV - 1,
        ],
        axis=1,
    )
    match = (
        neighbours[:, :, None] == jnp.arange(coarse_order.shape[0], dtype=jnp.int32)[None, None, :]
    )
    column_block = jnp.sum(jnp.where(match, coarse_order[None, None, :], 0), axis=-1)
    rows, select, share = panel_rows(blocks, column_block, present)
    assembled = lax.psum(share, ("row", "col"))
    panel = finish(rows, select, assembled)
    return (blocks.reshape(SUB_DEV, 7, NV * NV), panel)


def solution(mesh):
    in_specs = (
        P("row", "col", None, None),
        P("row", "col", None),
        P(),
        P("row", "col", None),
        P("row", "col", None),
        P("row", "col", None),
        P(),
    )
    out_specs = (P(("row", "col"), None, None), P(("row", "col"), None, None))
    return jax.shard_map(shards, mesh=mesh, in_specs=in_specs, out_specs=out_specs, check_vma=False)
```

profile of v0, /device:TPU:6, one launch (start us, length us, event | category | flops | bytes accessed | tf_op | source)
XLA Modules:
  0.0 590.4 jit_solution(2413078286542607056)
XLA Ops:
  7.2 2.8 fusion.121
  10.0 1.9 collective-permute-start
  11.9 3.6 collective-permute-start.1
  15.6 5.4 reshape.330
  21.0 2.6 fusion.118
  23.6 2.6 convert_subtract_fusion
  26.1 4.1 fusion.119
  30.8 5.3 reshape.326
  36.5 5.3 multiply_convert_fusion
  44.0 4.5 fusion.117
  52.7 1.5 copy.257
  57.8 4.5 convolution_bitcast_fusion.12
  62.3 1.6 convolution_bitcast_fusion.13
  65.5 2.2 copy.265
  70.2 1.8 slice_bitcast_fusion.1
  73.7 1.6 copy_convert_fusion
  77.2 2.0 multiply_convert_fusion.2
  79.9 2.9 copy.249
  82.8 1.6 copy.253
  84.4 1.6 copy.245
  86.2 3.1 convolution_bitcast_fusion.1
  89.4 6.7 %reshape_squeeze.26 = bf16[8,16,4,4,4,48]{5,4,3,2,1,0:T(4,128)(2,1)} reshape(bf16[1,8,16,3072]{3,2,1,0:T(8,128)(2,1)} %collective-permute-done) | data formatting | bytes 1572864 | tf_op jit(solution)/shard_map/reshape;squeeze | solution.py:36
  100.9 6.2 %reshape_squeeze.27 = bf16[8,16,4,4,4,48]{5,4,3,2,1,0:T(4,128)(2,1)} reshape(bf16[1,8,16,3072]{3,2,1,0:T(8,128)(2,1)} %collective-permute-done.1) | data formatting | bytes 1572864 | tf_op jit(solution)/shard_map/reshape;squeeze | solution.py:36
  111.2 1.3 constant_dynamic-update-slice_fusion.2
  115.0 4.7 collective-permute-start.2
  119.7 1.5 collective-permute-start.3
  122.8 1.5 bitcast_dynamic-update-slice_fusion.7
  129.0 3.3 collective-permute-done.3
  140.9 1.6 copy.281
  145.4 259.5 %all-reduce.7.cloned.1.call-done = f32[528,528]{0,1:T(8,128)} async-done(((f32[528,528]{0,1:T(8,128)}), f32[528,528]{0,1:T(8,128)}) %all-reduce.7.cloned.1.call-update) | async-done | bytes 1115152 | tf_op jit(solution)/shard_map/psum | solution.py:207
  404.9 3.0 copy.282
  407.9 1.5 fusion.3
  411.2 11.9 %cholesky.134 = f32[128,128]{1,0:T(8,128)S(1)} custom-call(f32[128,128]{1,0:T(8,128)S(1)} %cholesky.346), custom_call_target="Cholesky" | custom-call | tf_op jit(solution)/shard_map/jit(cholesky)/cholesky | solution.py:131
  423.2 9.8 %custom-call.39 = f32[1,128,128]{1,2,0:T(8,128)S(1)} custom-call(f32[1,128,128]{2,1,0:T(8,128)S(1)} %get-tuple-element.54), custom_call_target="InvertDiagBlocksLowerTriangular" | custom-call | tf_op jit(solution)/shard_map/jit(cholesky)/cholesky | solution.py:131
  435.6 11.7 %cholesky.274 = f32[128,128]{1,0:T(8,128)S(1)} custom-call(f32[128,128]{1,0:T(8,128)S(1)} %cholesky.350), custom_call_target="Cholesky" | custom-call | tf_op jit(solution)/shard_map/jit(cholesky)/cholesky | solution.py:131
  448.7 9.8 %custom-call.40 = f32[1,128,128]{1,2,0:T(8,128)S(1)} custom-call(f32[1,128,128]{2,1,0:T(8,128)S(1)} %get-tuple-element.51), custom_call_target="InvertDiagBlocksLowerTriangular" | custom-call | tf_op jit(solution)/shard_map/jit(cholesky)/cholesky | solution.py:131
  460.1 12.1 %cholesky.295 = f32[128,128]{1,0:T(8,128)S(1)} custom-call(f32[128,128]{1,0:T(8,128)S(1)} %cholesky.355), custom_call_target="Cholesky" | custom-call | tf_op jit(solution)/shard_map/jit(cholesky)/cholesky | solution.py:131
  472.8 9.8 %custom-call.41 = f32[1,128,128]{1,2,0:T(8,128)S(1)} custom-call(f32[1,128,128]{2,1,0:T(8,128)S(1)} %get-tuple-element.48), custom_call_target="InvertDiagBlocksLowerTriangular" | custom-call | tf_op jit(solution)/shard_map/jit(cholesky)/cholesky | solution.py:131
  484.1 11.7 %cholesky.314 = f32[128,128]{1,0:T(8,128)S(1)} custom-call(f32[128,128]{1,0:T(8,128)S(1)} %cholesky.360), custom_call_target="Cholesky" | custom-call | tf_op jit(solution)/shard_map/jit(cholesky)/cholesky | solution.py:131
  496.5 9.8 %custom-call.42 = f32[1,128,128]{1,2,0:T(8,128)S(1)} custom-call(f32[1,128,128]{2,1,0:T(8,128)S(1)} %get-tuple-element.45), custom_call_target="InvertDiagBlocksLowerTriangular" | custom-call | tf_op jit(solution)/shard_map/jit(cholesky)/cholesky | solution.py:131
  507.4 1.5 cholesky.334
  514.0 11.9 %while.1 = (s32[]{:T(128)}, f32[528,528]{1,0:T(8,128)}, s32[4,2]{0,1:T(2,128)S(1)}, f32[4,128,128]{2,1,0:T(8,128)S(1)}, s32[]{:T(128)}) while((s32[]{:T(128)}, f32[528,528]{1,0:T(8,128)}, s32[4,2]{0,1:T(2,128)S(1)}, f32[4,128,128]{2,1,0:T(8,128)S(1)}, s32[]{:T(128)}) %tuple.72), condition=%wide.while_cond, body=%wide.while_body.sunk | while | flops 2 | bytes 131181 | solution.py:133
  514.8 2.3 bitcast_dynamic-update-slice_fusion.9
  517.8 2.3 bitcast_dynamic-update-slice_fusion.9
  520.7 2.3 bitcast_dynamic-update-slice_fusion.9
  523.6 2.3 bitcast_dynamic-update-slice_fusion.9
  526.0 49.1 %custom-call.43 = f32[5,128,128]{1,2,0:T(8,128)S(1)} custom-call(f32[5,128,128]{2,1,0:T(8,128)S(1)} %pad_maximum_fusion), custom_call_target="InvertDiagBlocksLowerTriangular" | custom-call | tf_op jit(solution)/shard_map/jit(_solve_triangular)/triangular_solve | solution.py:133
  578.3 1.3 convolution_subtract_fusion.4
  (284 shorter events, 70.8 us)
Async XLA Ops:
  7.2 8.4 %copy-start.3 = (bf16[2,8,16,3072]{3,2,1,0:T(8,128)(2,1)S(1)}, bf16[2,8,16,3072]{3,2,1,0:T(8,128)(2,1)}, u32[]{:S(2)}) copy-start(bf16[2,8,16,3072]{3,2,1,0:T(8,128)(2,1)} %param.8) | copy-start | bytes 4718596
  7.2 397.8 %all-reduce.7.cloned.1.call-start = ((), (), s32[]{:S(2)}) async-start(), calls=%async_computation | async-start | bytes 2703360 | tf_op jit(solution)/shard_map/psum | solution.py:207
  10.0 79.4 %collective-permute-start = (bf16[1,8,16,3072]{3,2,1,0:T(8,128)(2,1)}, bf16[1,8,16,3072]{3,2,1,0:T(8,128)(2,1)}, u32[]{:S(2)}, u32[]{:S(2)}) collective-permute-start(bf16[1,8,16,3072]{3,2,1,0:T(8,128)(2,1)} %get-tuple-element.43), channel_id=1, source_target_pairs={{0,32},{32,64},{64,96},{96,128},{128,160},{160,192},{192,224},{1,3... | collective-permute-start | bytes 2359304 | tf_op jit(solution)/shard_map/ppermute | solution.py:19
  11.9 88.9 %collective-permute-start.1 = (bf16[1,8,16,3072]{3,2,1,0:T(8,128)(2,1)}, bf16[1,8,16,3072]{3,2,1,0:T(8,128)(2,1)}, u32[]{:S(2)}, u32[]{:S(2)}) collective-permute-start(bf16[1,8,16,3072]{3,2,1,0:T(8,128)(2,1)} %get-tuple-element.42), channel_id=1, source_target_pairs={{32,0},{64,32},{96,64},{128,96},{160,128},{192,160},{224,192},{33,... | collective-permute-start | bytes 2359304 | tf_op jit(solution)/shard_map/ppermute | solution.py:20
  26.1 4.1 copy-start.40
  30.3 5.8 copy-start.36
  30.8 5.3 copy-start.45
  30.8 5.5 copy-start.41
  30.8 5.7 copy-start.35
  36.5 5.3 copy-start
  41.8 2.2 copy-start.2
  44.0 8.1 %copy-start.39 = (f32[3,8,16]{2,1,0:T(8,128)S(1)}, f32[3,8,16]{2,1,0:T(8,128)}, u32[]{:S(2)}) copy-start(f32[3,8,16]{2,1,0:T(8,128)} %param.11) | copy-start | bytes 4612
  52.1 2.1 copy-start.12
  65.1 4.1 copy-start.19
  65.5 2.2 copy-start.42
  67.7 4.3 copy-start.54
  67.7 4.3 copy-start.55
  67.7 4.3 copy-start.56
  67.7 4.3 copy-start.57
  67.7 4.3 copy-start.58
  67.7 4.3 copy-start.59
  67.7 4.3 copy-start.60
  67.7 4.3 copy-start.46
  67.7 4.7 copy-start.34
  67.7 6.0 %copy-start.17 = (bf16[1,8,16,1,4,4,48]{6,5,4,3,2,1,0:T(4,128)(2,1)S(1)}, bf16[1,8,16,1,4,4,48]{6,5,4,3,2,1,0:T(4,128)(2,1)}, u32[]{:S(2)}) copy-start(bf16[1,8,16,1,4,4,48]{6,5,4,3,2,1,0:T(4,128)(2,1)} %get-tuple-element.36) | copy-start | bytes 589828
  67.8 6.0 %copy-start.18 = (bf16[1,8,16,1,4,4,48]{6,5,4,3,2,1,0:T(4,128)(2,1)S(1)}, bf16[1,8,16,1,4,4,48]{6,5,4,3,2,1,0:T(4,128)(2,1)}, u32[]{:S(2)}) copy-start(bf16[1,8,16,1,4,4,48]{6,5,4,3,2,1,0:T(4,128)(2,1)} %get-tuple-element.37) | copy-start | bytes 589828
  67.9 2.3 copy-start.32
  70.2 5.5 copy-start.15
  70.2 5.8 copy-start.21
  72.4 3.0 copy-start.38
  72.4 3.0 copy-start.50
  73.7 3.4 copy-start.1
  79.9 2.9 copy-start.8
  112.8 8.4 %copy-start.20 = (f32[1,8,16,1,4,4,48]{6,1,5,4,2,3,0:T(8,128)S(1)}, f32[1,8,16,1,4,4,48]{6,1,5,4,2,3,0:T(8,128)}, u32[]{:S(2)}) copy-start(f32[1,8,16,1,4,4,48]{6,1,5,4,2,3,0:T(8,128)} %copy.245) | copy-start | bytes 1179652
  112.8 8.4 %copy-start.43 = (f32[1,8,16]{1,2,0:T(8,128)S(1)}, f32[1,8,16]{1,2,0:T(8,128)}, u32[]{:S(2)}) copy-start(f32[1,8,16]{1,2,0:T(8,128)} %get-tuple-element.55) | copy-start | bytes 1540
  112.8 8.4 %copy-start.64 = (f32[4,48,48]{2,1,0:T(8,128)S(1)}, f32[4,48,48]{2,1,0:T(8,128)}, u32[]{:S(2)}) copy-start(f32[4,48,48]{2,1,0:T(8,128)} %convolution_bitcast_fusion.10) | copy-start | bytes 110596
  115.0 6.7 %copy-start.28 = (f32[4,48,48]{2,1,0:T(8,128)S(1)}, f32[4,48,48]{2,1,0:T(8,128)}, u32[]{:S(2)}) copy-start(f32[4,48,48]{2,1,0:T(8,128)} %convolution_bitcast_fusion.12) | copy-start | bytes 110596
  115.0 6.7 %copy-start.29 = (f32[4,48,48]{2,1,0:T(8,128)S(1)}, f32[4,48,48]{2,1,0:T(8,128)}, u32[]{:S(2)}) copy-start(f32[4,48,48]{2,1,0:T(8,128)} %convolution_bitcast_fusion.13) | copy-start | bytes 110596
  115.0 6.7 %copy-start.33 = (f32[4,48,48]{2,1,0:T(8,128)S(1)}, f32[4,48,48]{2,1,0:T(8,128)}, u32[]{:S(2)}) copy-start(f32[4,48,48]{2,1,0:T(8,128)} %fusion.24) | copy-start | bytes 110596
  115.0 12.5 %collective-permute-start.2 = (bf16[4,1,16,3072]{3,2,1,0:T(8,128)(2,1)}, bf16[4,1,16,3072]{3,2,1,0:T(8,128)(2,1)}, u32[]{:S(2)}, u32[]{:S(2)}) collective-permute-start(bf16[4,1,16,3072]{3,2,1,0:T(8,128)(2,1)} %get-tuple-element.41), channel_id=1, source_target_pairs={{0,1},{1,2},{2,3},{3,4},{4,5},{5,6},{6,7},{7,8},{8,9},{9,10},{10,1... | collective-permute-start | bytes 1179656 | tf_op jit(solution)/shard_map/ppermute | solution.py:19
  119.7 12.6 %collective-permute-start.3 = (bf16[4,1,16,3072]{3,2,1,0:T(8,128)(2,1)}, bf16[4,1,16,3072]{3,2,1,0:T(8,128)(2,1)}, u32[]{:S(2)}, u32[]{:S(2)}) collective-permute-start(bf16[4,1,16,3072]{3,2,1,0:T(8,128)(2,1)} %get-tuple-element.40), channel_id=1, source_target_pairs={{1,0},{2,1},{3,2},{4,3},{5,4},{6,5},{7,6},{8,7},{9,8},{10,9},{11,1... | collective-permute-start | bytes 1179656 | tf_op jit(solution)/shard_map/ppermute | solution.py:20
  125.8 8.1 %copy-start.16 = (f32[1,2,16,16,48]{4,2,3,0,1:T(8,128)S(1)}, f32[1,2,16,16,48]{4,2,3,0,1:T(8,128)}, u32[]{:S(2)}) copy-start(f32[1,2,16,16,48]{4,2,3,0,1:T(8,128)} %slice_convert_fusion.1) | copy-start | bytes 294916
  129.0 5.6 slice-start
  133.8 2.0 slice-start.1
  133.9 2.0 copy-start.48
  404.9 3.0 copy-start.7
  512.7 13.2 %copy-start.31 = (f32[128,112]{1,0:T(8,128)S(1)}, f32[128,112]{1,0:T(8,128)}, u32[]{:S(2)}) copy-start(f32[128,112]{1,0:T(8,128)} %pad_convert_fusion) | copy-start | bytes 172036
  576.5 4.8 copy-start.61
  (26 other events, 34.9 us)
Sparse Core Ops, SparseCore 0:
  142.6 262.2 all-reduce.6
where the time goes:
time: 597 us; the launch traced here: 590 us
  waiting for transfers between devices  264 us (44%)
  other arithmetic  157 us (26%)
  local copies, waits for them, and re-layouts  95.1 us (16%)
  matrix products  44.6 us (7%)
  between operations  18.6 us (3%)
  starting transfers between devices  11.8 us (2%)
    psum x1, waiting for transfers between devices, shards(): assembled = lax.psum(share, ('row', 'col'))  259 us
    another operation x19, other arithmetic, finish(): factor = jnp.linalg.cholesky(0.5 * (whole + whole.T))  91.6 us
    another operation x7, other arithmetic, finish(): jax.scipy.linalg.solve_triangular(factor, rows.reshape(count * NV, PB * N...  50.7 us
    dot_general x21, matrix products, contract(): return jnp.einsum(form, left, right, preferred_element_type=jnp.float32)  28.5 us
    slice x10, local copies, waits for them, and re-layouts, traces(): picked = lax.index_in_dim(nodes, side, lead + axis, keepdims=False)  16.6 us
    another operation x4, local copies, waits for them, and re-layouts, traces(): nodes = values.reshape(values.shape[:lead] + (4, 4, 4, NV))  14 us
    unnamed x143, local copies, waits for them, and re-layouts  12.1 us
  transfers between devices with their start and end apart: 5, of which 3 were waited for; matrix products, arithmetic and copies ran while one was open for 15% of the time, Pallas kernels for 0%

commit v1 on v0

--- a/solution.py
+++ b/solution.py
@@ -7,6 +7,7 @@
 SUB_DEV = 4
 PB = 11
 LINE_WEIGHTS = (1.0 / 6.0, 5.0 / 6.0, 5.0 / 6.0, 1.0 / 6.0)
+_apply_stops_all = lambda local_array: lax.psum(lax.psum(local_array, axis_name="col"), "row")
 
 
 def with_halo(shard, sides, width):
@@ -204,7 +205,7 @@
     )
     column_block = jnp.sum(jnp.where(match, coarse_order[None, None, :], 0), axis=-1)
     rows, select, share = panel_rows(blocks, column_block, present)
-    assembled = lax.psum(share, ("row", "col"))
+    assembled = _apply_stops_all(share)
     panel = finish(rows, select, assembled)
     return (blocks.reshape(SUB_DEV, 7, NV * NV), panel)
 

time: 597 us -> 557 us (0.933)
  waiting for transfers between devices: 264 us -> 222 us
    psum x1 -> x2, waiting for transfers between devices: 259 us -> 216 us  [the longest x1 153 us: lax.psum(local_array, axis_name='col')]
    unnamed x143 -> x141, local copies, waits for them, and re-layouts: 12.1 us -> 10.4 us
  transfers between devices with their start and end apart: 5 -> 6, of which waited for: 3 -> 4; matrix products, arithmetic and copies ran while one was open for 15% -> 16% of each run, Pallas kernels for 0% -> 0%
where the time goes in v1:
time: 557 us; the launch traced here: 547 us
  waiting for transfers between devices  222 us (40%)
  other arithmetic  156 us (28%)
  local copies, waits for them, and re-layouts  93.3 us (17%)
  matrix products  45.4 us (8%)
  between operations  19 us (3%)
  starting transfers between devices  11.8 us (2%)
    psum x1, waiting for transfers between devices, lax.psum(local_array, axis_name='col')  153 us
    another operation x19, other arithmetic, finish(): factor = jnp.linalg.cholesky(0.5 * (whole + whole.T))  91.6 us
    psum x1, waiting for transfers between devices, lax.psum(lax.psum(local_array, axis_name='col'), 'row')  63.1 us
    another operation x7, other arithmetic, finish(): jax.scipy.linalg.solve_triangular(factor, rows.reshape(count * NV, PB * N...  51.2 us
    dot_general x21, matrix products, contract(): return jnp.einsum(form, left, right, preferred_element_type=jnp.float32)  27.9 us
    slice x10, local copies, waits for them, and re-layouts, traces(): picked = lax.index_in_dim(nodes, side, lead + axis, keepdims=False)  16.5 us
    another operation x4, local copies, waits for them, and re-layouts, traces(): nodes = values.reshape(values.shape[:lead] + (4, 4, 4, NV))  13.9 us
    another operation x13, local copies, waits for them, and re-layouts  12 us
  transfers between devices with their start and end apart: 6, of which 4 were waited for; matrix products, arithmetic and copies ran while one was open for 16% of the time, Pallas kernels for 0%

profile of v1, /device:TPU:6, one launch (start us, length us, event | category | flops | bytes accessed | tf_op | source)
XLA Modules:
  0.0 547.3 jit_solution(5035964121212085930)
XLA Ops:
  7.2 2.8 fusion.121
  10.0 1.9 collective-permute-start
  11.9 3.6 collective-permute-start.1
  15.6 5.4 reshape.330
  21.0 2.6 fusion.118
  23.6 2.6 convert_subtract_fusion
  26.1 4.1 fusion.119
  30.3 5.3 reshape.326
  36.0 5.3 multiply_convert_fusion
  43.5 4.5 fusion.117
  52.1 1.5 copy.257
  56.5 4.4 convolution_bitcast_fusion.12
  61.0 1.6 convolution_bitcast_fusion.13
  64.2 2.2 copy.265
  68.9 1.8 slice_bitcast_fusion.1
  72.4 1.6 copy_convert_fusion
  75.8 2.0 multiply_convert_fusion.2
  78.4 2.9 copy.249
  81.3 1.6 copy.253
  82.9 1.6 copy.245
  85.3 3.3 convolution_bitcast_fusion.1
  88.6 6.6 %reshape_squeeze.26 = bf16[8,16,4,4,4,48]{5,4,3,2,1,0:T(4,128)(2,1)} reshape(bf16[1,8,16,3072]{3,2,1,0:T(8,128)(2,1)} %collective-permute-done) | data formatting | bytes 1572864 | tf_op jit(solution)/shard_map/reshape;squeeze | solution.py:37
  99.4 6.2 %reshape_squeeze.27 = bf16[8,16,4,4,4,48]{5,4,3,2,1,0:T(4,128)(2,1)} reshape(bf16[1,8,16,3072]{3,2,1,0:T(8,128)(2,1)} %collective-permute-done.1) | data formatting | bytes 1572864 | tf_op jit(solution)/shard_map/reshape;squeeze | solution.py:37
  112.0 4.7 collective-permute-start.2
  122.6 1.9 collective-permute-done.2
  126.0 3.3 collective-permute-done.3
  135.9 2.4 fusion.33
  140.4 153.3 %all-reduce.8.cloned.1.call-done = f32[11,48,528]{2,0,1:T(8,128)} async-done(((f32[11,48,528]{2,0,1:T(8,128)}), f32[11,48,528]{2,0,1:T(8,128)}) %all-reduce.8.cloned.1.call-update) | async-done | bytes 1115152 | tf_op jit(solution)/shard_map/psum | solution.py:10
  293.8 2.0 copy.280
  295.8 1.6 copy.281
  298.1 63.1 %all-reduce.10.cloned.1.call-done = f32[528,528]{0,1:T(8,128)} async-done(((f32[528,528]{0,1:T(8,128)}), f32[528,528]{0,1:T(8,128)}) %all-reduce.10.cloned.1.call-update) | async-done | bytes 1115152 | tf_op jit(solution)/shard_map/psum | solution.py:10
  361.2 3.0 copy.282
  364.2 1.5 fusion.3
  367.5 11.7 %cholesky.134 = f32[128,128]{1,0:T(8,128)S(1)} custom-call(f32[128,128]{1,0:T(8,128)S(1)} %cholesky.346), custom_call_target="Cholesky" | custom-call | tf_op jit(solution)/shard_map/jit(cholesky)/cholesky | solution.py:132
  379.3 9.8 %custom-call.39 = f32[1,128,128]{1,2,0:T(8,128)S(1)} custom-call(f32[1,128,128]{2,1,0:T(8,128)S(1)} %get-tuple-element.54), custom_call_target="InvertDiagBlocksLowerTriangular" | custom-call | tf_op jit(solution)/shard_map/jit(cholesky)/cholesky | solution.py:132
  391.7 11.9 %cholesky.274 = f32[128,128]{1,0:T(8,128)S(1)} custom-call(f32[128,128]{1,0:T(8,128)S(1)} %cholesky.350), custom_call_target="Cholesky" | custom-call | tf_op jit(solution)/shard_map/jit(cholesky)/cholesky | solution.py:132
  405.0 9.8 %custom-call.40 = f32[1,128,128]{1,2,0:T(8,128)S(1)} custom-call(f32[1,128,128]{2,1,0:T(8,128)S(1)} %get-tuple-element.51), custom_call_target="InvertDiagBlocksLowerTriangular" | custom-call | tf_op jit(solution)/shard_map/jit(cholesky)/cholesky | solution.py:132
  416.4 11.7 %cholesky.295 = f32[128,128]{1,0:T(8,128)S(1)} custom-call(f32[128,128]{1,0:T(8,128)S(1)} %cholesky.355), custom_call_target="Cholesky" | custom-call | tf_op jit(solution)/shard_map/jit(cholesky)/cholesky | solution.py:132
  428.8 9.8 %custom-call.41 = f32[1,128,128]{1,2,0:T(8,128)S(1)} custom-call(f32[1,128,128]{2,1,0:T(8,128)S(1)} %get-tuple-element.48), custom_call_target="InvertDiagBlocksLowerTriangular" | custom-call | tf_op jit(solution)/shard_map/jit(cholesky)/cholesky | solution.py:132
  440.2 11.9 %cholesky.314 = f32[128,128]{1,0:T(8,128)S(1)} custom-call(f32[128,128]{1,0:T(8,128)S(1)} %cholesky.360), custom_call_target="Cholesky" | custom-call | tf_op jit(solution)/shard_map/jit(cholesky)/cholesky | solution.py:132
  452.8 9.8 %custom-call.42 = f32[1,128,128]{1,2,0:T(8,128)S(1)} custom-call(f32[1,128,128]{2,1,0:T(8,128)S(1)} %get-tuple-element.45), custom_call_target="InvertDiagBlocksLowerTriangular" | custom-call | tf_op jit(solution)/shard_map/jit(cholesky)/cholesky | solution.py:132
  463.6 1.5 cholesky.334
  470.4 12.1 %while.1 = (s32[]{:T(128)}, f32[528,528]{1,0:T(8,128)}, s32[4,2]{0,1:T(2,128)S(1)}, f32[4,128,128]{2,1,0:T(8,128)S(1)}, s32[]{:T(128)}) while((s32[]{:T(128)}, f32[528,528]{1,0:T(8,128)}, s32[4,2]{0,1:T(2,128)S(1)}, f32[4,128,128]{2,1,0:T(8,128)S(1)}, s32[]{:T(128)}) %tuple.74), condition=%wide.while_cond, body=%wide.while_body.sunk | while | flops 2 | bytes 131181 | solution.py:134
  471.1 2.3 bitcast_dynamic-update-slice_fusion.9
  474.1 2.3 bitcast_dynamic-update-slice_fusion.9
  477.2 2.3 bitcast_dynamic-update-slice_fusion.9
  480.2 2.3 bitcast_dynamic-update-slice_fusion.9
  482.7 49.1 %custom-call.43 = f32[5,128,128]{1,2,0:T(8,128)S(1)} custom-call(f32[5,128,128]{2,1,0:T(8,128)S(1)} %pad_maximum_fusion), custom_call_target="InvertDiagBlocksLowerTriangular" | custom-call | tf_op jit(solution)/shard_map/jit(_solve_triangular)/triangular_solve | solution.py:134
  (285 shorter events, 69.6 us)
Async XLA Ops:
  7.2 8.4 %copy-start.3 = (bf16[2,8,16,3072]{3,2,1,0:T(8,128)(2,1)S(1)}, bf16[2,8,16,3072]{3,2,1,0:T(8,128)(2,1)}, u32[]{:S(2)}) copy-start(bf16[2,8,16,3072]{3,2,1,0:T(8,128)(2,1)} %param.8) | copy-start | bytes 4718596
  7.2 286.6 %all-reduce.8.cloned.1.call-start = ((), (), s32[]{:S(2)}) async-start(), calls=%async_computation | async-start | bytes 3932160 | tf_op jit(solution)/shard_map/psum | solution.py:10
  10.0 78.6 %collective-permute-start = (bf16[1,8,16,3072]{3,2,1,0:T(8,128)(2,1)}, bf16[1,8,16,3072]{3,2,1,0:T(8,128)(2,1)}, u32[]{:S(2)}, u32[]{:S(2)}) collective-permute-start(bf16[1,8,16,3072]{3,2,1,0:T(8,128)(2,1)} %get-tuple-element.43), channel_id=1, source_target_pairs={{0,32},{32,64},{64,96},{96,128},{128,160},{160,192},{192,224},{1,3... | collective-permute-start | bytes 2359304 | tf_op jit(solution)/shard_map/ppermute | solution.py:20
  11.9 87.4 %collective-permute-start.1 = (bf16[1,8,16,3072]{3,2,1,0:T(8,128)(2,1)}, bf16[1,8,16,3072]{3,2,1,0:T(8,128)(2,1)}, u32[]{:S(2)}, u32[]{:S(2)}) collective-permute-start(bf16[1,8,16,3072]{3,2,1,0:T(8,128)(2,1)} %get-tuple-element.42), channel_id=1, source_target_pairs={{32,0},{64,32},{96,64},{128,96},{160,128},{192,160},{224,192},{33,... | collective-permute-start | bytes 2359304 | tf_op jit(solution)/shard_map/ppermute | solution.py:21
  26.1 4.1 copy-start.37
  30.3 5.4 copy-start.33
  30.3 5.3 copy-start.43
  30.3 5.6 %copy-start.38 = (f32[2,8,16]{2,1,0:T(8,128)S(1)}, f32[2,8,16]{2,1,0:T(8,128)}, u32[]{:S(2)}) copy-start(f32[2,8,16]{2,1,0:T(8,128)} %param.9) | copy-start | bytes 3076
  30.3 5.7 %copy-start.32 = (bf16[3,64,64]{2,1,0:T(8,128)(2,1)S(1)}, bf16[3,64,64]{2,1,0:T(8,128)(2,1)}, u32[]{:S(2)}) copy-start(bf16[3,64,64]{2,1,0:T(8,128)(2,1)} %param.10) | copy-start | bytes 73732
  36.0 5.3 copy-start
  41.3 2.2 copy-start.2
  43.5 7.9 %copy-start.36 = (f32[3,8,16]{2,1,0:T(8,128)S(1)}, f32[3,8,16]{2,1,0:T(8,128)}, u32[]{:S(2)}) copy-start(f32[3,8,16]{2,1,0:T(8,128)} %param.11) | copy-start | bytes 4612
  51.5 2.2 copy-start.12
  63.8 4.1 copy-start.19
  64.2 2.2 copy-start.39
  66.4 4.3 copy-start.54
  66.4 4.3 copy-start.55
  66.4 4.3 copy-start.56
  66.4 4.3 copy-start.57
  66.4 4.3 copy-start.58
  66.4 4.3 copy-start.59
  66.4 4.3 copy-start.44
  66.4 4.6 copy-start.31
  66.4 5.9 %copy-start.17 = (bf16[1,8,16,1,4,4,48]{6,5,4,3,2,1,0:T(4,128)(2,1)S(1)}, bf16[1,8,16,1,4,4,48]{6,5,4,3,2,1,0:T(4,128)(2,1)}, u32[]{:S(2)}) copy-start(bf16[1,8,16,1,4,4,48]{6,5,4,3,2,1,0:T(4,128)(2,1)} %get-tuple-element.36) | copy-start | bytes 589828
  66.5 5.9 %copy-start.18 = (bf16[1,8,16,1,4,4,48]{6,5,4,3,2,1,0:T(4,128)(2,1)S(1)}, bf16[1,8,16,1,4,4,48]{6,5,4,3,2,1,0:T(4,128)(2,1)}, u32[]{:S(2)}) copy-start(bf16[1,8,16,1,4,4,48]{6,5,4,3,2,1,0:T(4,128)(2,1)} %get-tuple-element.37) | copy-start | bytes 589828
  66.6 2.3 copy-start.29
  67.2 3.5 copy-start.45
  68.9 5.4 copy-start.15
  68.9 5.7 %copy-start.21 = (bf16[7,2,16,16,48]{4,2,3,0,1:T(8,128)(2,1)S(1)}, bf16[7,2,16,16,48]{4,2,3,0,1:T(8,128)(2,1)}, u32[]{:S(2)}) copy-start(bf16[7,2,16,16,48]{4,2,3,0,1:T(8,128)(2,1)} %multiply_convert_fusion.3) | copy-start | bytes 1032196
  71.1 2.9 copy-start.50
  72.4 3.4 copy-start.1
  78.4 2.9 copy-start.8
  109.7 8.3 %copy-start.20 = (f32[1,8,16,1,4,4,48]{6,1,5,4,2,3,0:T(8,128)S(1)}, f32[1,8,16,1,4,4,48]{6,1,5,4,2,3,0:T(8,128)}, u32[]{:S(2)}) copy-start(f32[1,8,16,1,4,4,48]{6,1,5,4,2,3,0:T(8,128)} %copy.245) | copy-start | bytes 1179652
  109.7 8.3 %copy-start.40 = (f32[1,8,16]{1,2,0:T(8,128)S(1)}, f32[1,8,16]{1,2,0:T(8,128)}, u32[]{:S(2)}) copy-start(f32[1,8,16]{1,2,0:T(8,128)} %get-tuple-element.55) | copy-start | bytes 1540
  112.0 6.5 %copy-start.25 = (f32[4,48,48]{2,1,0:T(8,128)S(1)}, f32[4,48,48]{2,1,0:T(8,128)}, u32[]{:S(2)}) copy-start(f32[4,48,48]{2,1,0:T(8,128)} %convolution_bitcast_fusion.12) | copy-start | bytes 110596
  112.0 6.5 %copy-start.26 = (f32[4,48,48]{2,1,0:T(8,128)S(1)}, f32[4,48,48]{2,1,0:T(8,128)}, u32[]{:S(2)}) copy-start(f32[4,48,48]{2,1,0:T(8,128)} %convolution_bitcast_fusion.13) | copy-start | bytes 110596
  112.0 6.5 %copy-start.30 = (f32[4,48,48]{2,1,0:T(8,128)S(1)}, f32[4,48,48]{2,1,0:T(8,128)}, u32[]{:S(2)}) copy-start(f32[4,48,48]{2,1,0:T(8,128)} %fusion.24) | copy-start | bytes 110596
  112.0 12.5 %collective-permute-start.2 = (bf16[4,1,16,3072]{3,2,1,0:T(8,128)(2,1)}, bf16[4,1,16,3072]{3,2,1,0:T(8,128)(2,1)}, u32[]{:S(2)}, u32[]{:S(2)}) collective-permute-start(bf16[4,1,16,3072]{3,2,1,0:T(8,128)(2,1)} %get-tuple-element.41), channel_id=1, source_target_pairs={{0,1},{1,2},{2,3},{3,4},{4,5},{5,6},{6,7},{7,8},{8,9},{9,10},{10,1... | collective-permute-start | bytes 1179656 | tf_op jit(solution)/shard_map/ppermute | solution.py:20
  116.7 12.6 %collective-permute-start.3 = (bf16[4,1,16,3072]{3,2,1,0:T(8,128)(2,1)}, bf16[4,1,16,3072]{3,2,1,0:T(8,128)(2,1)}, u32[]{:S(2)}, u32[]{:S(2)}) collective-permute-start(bf16[4,1,16,3072]{3,2,1,0:T(8,128)(2,1)} %get-tuple-element.40), channel_id=1, source_target_pairs={{1,0},{2,1},{3,2},{4,3},{5,4},{6,5},{7,6},{8,7},{9,8},{10,9},{11,1... | collective-permute-start | bytes 1179656 | tf_op jit(solution)/shard_map/ppermute | solution.py:21
  121.7 9.2 %copy-start.16 = (f32[1,2,16,16,48]{4,2,3,0,1:T(8,128)S(1)}, f32[1,2,16,16,48]{4,2,3,0,1:T(8,128)}, u32[]{:S(2)}) copy-start(f32[1,2,16,16,48]{4,2,3,0,1:T(8,128)} %slice_convert_fusion.1) | copy-start | bytes 294916
  125.9 5.6 %slice-start = ((bf16[2,8,4,16,48]{4,1,3,2,0:T(8,128)(2,1)}), bf16[2,8,3,16,48]{4,1,3,2,0:T(8,128)(2,1)S(1)}, s32[]{:S(2)}) async-start(bf16[2,8,4,16,48]{4,1,3,2,0:T(8,128)(2,1)} %slice_bitcast_fusion), calls=%async_computation.2 | async-start | bytes 393216 | tf_op jit(solution)/shard_map/slice | solution.py:88
  126.0 5.6 %copy-start.48 = (f32[2,8,4]{1,2,0:T(4,128)S(1)}, f32[2,8,4]{1,2,0:T(4,128)}, u32[]{:S(2)}) copy-start(f32[2,8,4]{1,2,0:T(4,128)} %get-tuple-element.66) | copy-start | bytes 772
  130.8 2.0 slice-start.1
  131.5 2.6 copy-start.49
  138.4 222.8 %all-reduce.10.cloned.1.call-start = ((), (), s32[]{:S(2)}) async-start(), calls=%async_computation.1 | async-start | bytes 2703360 | tf_op jit(solution)/shard_map/psum | solution.py:10
  361.2 3.0 copy-start.7
  469.1 13.4 %copy-start.28 = (f32[128,112]{1,0:T(8,128)S(1)}, f32[128,112]{1,0:T(8,128)}, u32[]{:S(2)}) copy-start(f32[128,112]{1,0:T(8,128)} %pad_convert_fusion) | copy-start | bytes 172036
  533.2 4.8 copy-start.60
  (26 other events, 35.4 us)
Sparse Core Ops, SparseCore 0:
  138.5 155.2 all-reduce.7
  297.5 63.7 all-reduce.9
